TPU v7x, 32 devices: a whole 2x2x4 slice. The times are simulated.
32 devices in a mesh: groups: 2 (over y), rows: 4 (over x, core), cols: 4 (over z).
Axes of the slice: x: 2, y: 2, z: 4, core: 2. Of those that a mesh axis runs over, the one named last changes fastest.
Arguments:
- pair_rep: float32 [384, 192, 128], P(('groups', 'cols'), 'rows'), parts along dimension 0, may hold values from -6 to 6
- token_mask: int32 [384], P(('groups', 'rows')), parts along dimension 0, may hold values from 0 to 1, as said below
- norm_gain: float32 [128], replicated, may hold values from 0.1 to 1.9
- norm_shift: float32 [128], replicated, may hold values from -3 to 3
- w_query: bfloat16 [128, 128], replicated, may hold values from -0.5 to 0.5
- w_keyval: bfloat16 [128, 256], replicated, may hold values from -0.5 to 0.5
- w_gate: bfloat16 [128, 128], replicated, may hold values from -0.5 to 0.5
- gate_shift: float32 [128], replicated, may hold values from -3 to 3
- w_bias: float32 [128, 4], replicated, may hold values from -12 to 12
- w_out: bfloat16 [128, 128], replicated, may hold values from -0.5 to 0.5
- out_shift: float32 [128], replicated, may hold values from -3 to 3
Outputs:
- pair_update: float32 [384, 192, 128], P(('groups', 'cols'), 'rows'), parts along dimension 0
There are 2 independent parts, one for each index of `groups`. A program takes and returns all parts, laid end to end along the dimension named above; an argument that names none is the same for every part. Nothing has to cross between parts.
Inputs may be any that keep to these rules, and one draw needn't show every extreme that they name: `token_mask`: position 0 is always a valid residue and the last position never is.
All inputs are finite; a program needn't handle non-finite values.
Results may differ from a plain program's by a relative error of at most 0.012.
The roundings to bfloat16 on the way count: a program that leaves them out, or rounds other values in their place, can miss the bound.
Values may be sent and summed in bfloat16 or wider, within the bound.
No kernel may reach another device: no remote copies, remote signals or barrier semaphores. Data moves between devices by JAX's collectives and lax.ppermute only.
A program may use at most 128 MiB of HBM per device.

v0:
```python
import jax
import jax.numpy as jnp
from jax import lax
from jax.sharding import PartitionSpec as P

HEADS = 4
HEAD_DIM = 32


def layer_norm(values, norm_gain, norm_shift):
    mean_val = jnp.mean(values, axis=-1, keepdims=True)
    centred = values - mean_val
    variance = jnp.mean(centred * centred, axis=-1, keepdims=True)
    return (centred * lax.rsqrt(variance + 1e-05) * norm_gain + norm_shift).astype(jnp.bfloat16)


def largest_divisor(count, limit):
    return max(
        (candidate for candidate in range(1, min(count, limit) + 1) if count % candidate == 0)
    )


def whole_row_layer(
    normed, token_mask, w_query, w_keyval, w_gate, gate_shift, w_bias, w_out, out_shift
):
    width = normed.shape[2]
    local_bias = jnp.dot(
        normed.astype(jnp.float32), w_bias, precision=lax.Precision.HIGHEST
    ).transpose(2, 0, 1)
    wide = lax.all_to_all(normed, "rows", split_axis=0, concat_axis=1, tiled=True)
    few_rows, token_count, _ = wide.shape
    bias_part = lax.all_gather(local_bias, "cols", axis=1, tiled=True)
    full_bias, full_mask = (
        lax.all_gather(bias_part, "rows", axis=2, tiled=True),
        lax.all_gather(token_mask.astype(jnp.float32), "rows", axis=0, tiled=True),
    )
    queries = (
        jnp.dot(wide, w_query, preferred_element_type=jnp.float32) * HEAD_DIM ** (-0.5)
    ).astype(jnp.bfloat16)
    queries = queries.reshape(few_rows, token_count, HEADS, HEAD_DIM)
    keyvals = jnp.dot(wide, w_keyval, preferred_element_type=jnp.float32).astype(jnp.bfloat16)
    keys = keyvals[..., :width].reshape(few_rows, token_count, HEADS, HEAD_DIM)
    values = keyvals[..., width:].reshape(few_rows, token_count, HEADS, HEAD_DIM)
    gates = jax.nn.sigmoid(jnp.dot(wide, w_gate, preferred_element_type=jnp.float32) + gate_shift)
    usable = full_mask > 0.5
    block_len = largest_divisor(token_count, 128)

    def one_block(block_index, gated_all):
        start = block_index * block_len
        query_block = lax.dynamic_slice_in_dim(queries, start, block_len, 1)
        bias_block = lax.dynamic_slice_in_dim(full_bias, start, block_len, 1)
        gate_block = lax.dynamic_slice_in_dim(gates, start, block_len, 1)
        scores = jnp.einsum(
            "ijhd,ikhd->hijk", query_block, keys, preferred_element_type=jnp.float32
        )
        scores = scores + bias_block[:, None]
        scores = jnp.where(usable[None, None, None, :], scores, jnp.float32(-1000000000.0))
        highest = jnp.max(scores, axis=-1, keepdims=True)
        expo = jnp.exp(scores - highest)
        total = jnp.sum(expo, axis=-1)
        weights = expo.astype(jnp.bfloat16)
        mixed = jnp.einsum("hijk,ikhd->ijhd", weights, values, preferred_element_type=jnp.float32)
        attended = mixed / total.transpose(1, 2, 0)[..., None]
        gated = (gate_block * attended.reshape(few_rows, block_len, width)).astype(jnp.bfloat16)
        return lax.dynamic_update_slice_in_dim(gated_all, gated, start, 1)

    gated_all = lax.fori_loop(
        0,
        token_count // block_len,
        one_block,
        jnp.zeros((few_rows, token_count, width), jnp.bfloat16),
    )
    gated_home = lax.all_to_all(gated_all, "rows", split_axis=1, concat_axis=0, tiled=True)
    return jnp.dot(gated_home, w_out, preferred_element_type=jnp.float32) + out_shift


def on_device(
    pair_rep,
    token_mask,
    norm_gain,
    norm_shift,
    w_query,
    w_keyval,
    w_gate,
    gate_shift,
    w_bias,
    w_out,
    out_shift,
):
    normed = layer_norm(pair_rep, norm_gain, norm_shift)
    return whole_row_layer(
        normed, token_mask, w_query, w_keyval, w_gate, gate_shift, w_bias, w_out, out_shift
    )


def solution(mesh):
    return jax.shard_map(
        on_device,
        mesh=mesh,
        in_specs=(
            P(("groups", "cols"), "rows", None),
            P(("groups", "rows")),
            P(),
            P(),
            P(),
            P(),
            P(),
            P(),
            P(),
            P(),
            P(),
        ),
        out_specs=P(("groups", "cols"), "rows", None),
        check_vma=False,
    )
```

profile of v0, /device:TPU:0, one launch (start us, length us, event | category | flops | bytes accessed | tf_op | source)
XLA Modules:
  0.0 85.9 jit_solution(3610924705760710887)
XLA Ops:
  0.0 1.7 %reduce_sum.31 = f32[48,48]{1,0:T(8,128)S(1)} reduce(f32[48,48,128]{2,1,0:T(8,128)} %param.13, f32[]{:T(128)} %constant.58.clone.1), dimensions={2}, to_apply=%region_0.0 | reduce | flops 292608 | bytes 1188868 | tf_op jit(solution)/shard_map/reduce_sum | solution.py:11
  1.8 0.7 multiply_reduce_fusion
  2.5 1.5 %add_convert_fusion = bf16[48,48,128]{2,1,0:T(8,128)(2,1)} fusion(f32[48,48,128]{2,1,0:T(8,128)S(1)} %copy-done.1, f32[128]{0:T(128)S(1)} %copy-done.8, f32[128]{0:T(128)S(1)} %copy-done.9, f32[48,48]{1,0:T(8,128)S(1)} %add_rsqrt_fusion, f32[48,48]{1,0:T(8,128)S(1)} %broadcast_multiply_fusion), kind=kLoop, calls=%fused_computation.31 | loop fusion | flops 1474560 | bytes 1788928 | tf_op jit(solution)/shard_map/convert_element_type | solution.py:14
  4.0 4.2 %all-to-all-start = ((bf16[48,48,128]{2,1,0:T(8,128)(2,1)}), bf16[48,48,128]{2,1,0:T(8,128)(2,1)S(1)}, u32[]{:S(2)}, u32[]{:S(2)}) async-start(bf16[48,48,128]{2,1,0:T(8,128)(2,1)} %add_convert_fusion), calls=%async_computation | async-start | bytes 1179648 | tf_op jit(solution)/shard_map/all_to_all | solution.py:30
  8.3 2.8 %convolution_bitcast_fusion = f32[4,48,48]{2,0,1:T(4,128)S(1)} fusion(bf16[48,48,128]{2,1,0:T(8,128)(2,1)} %add_convert_fusion, f32[128,4]{0,1:T(4,128)S(1)} %copy-done.7), kind=kOutput, calls=%fused_computation.33 | convolution fusion | flops 14155776 | bytes 628736 | tf_op jit(solution)/shard_map/dot_general | solution.py:27
  11.1 15.8 %all_gather.10 = f32[4,192,48]{2,0,1:T(4,128)S(1)} all-gather(f32[4,48,48]{2,0,1:T(4,128)S(1)} %convolution_bitcast_fusion), channel_id=1, replica_groups=mesh['groups'=2,'rows'=4,'cols'=4] {'cols'}, dimensions={1}, use_global_device_ids=true | all-gather | bytes 184320 | tf_op jit(solution)/shard_map/all_gather | solution.py:32
  27.2 0.6 dynamic-slice
  28.4 5.6 %all-reduce = f32[192]{0:T(256)S(1)} all-reduce(f32[192]{0:T(256)S(1)} %convert_dynamic-update-slice_fusion), channel_id=1, replica_groups=mesh['groups'=2,'rows'=4,'cols'=4] {'rows'}, use_global_device_ids=true, to_apply=%add | all-reduce | flops 192 | bytes 1536
  34.1 9.0 %all_gather.11 = f32[4,192,192]{1,0,2:T(4,128)S(1)} all-gather(f32[4,192,48]{1,0,2:T(4,128)S(1)} %copy.36), channel_id=1, replica_groups=mesh['groups'=2,'rows'=4,'cols'=4] {'rows'}, dimensions={2}, use_global_device_ids=true | all-gather | bytes 737280 | tf_op jit(solution)/shard_map/all_gather | solution.py:34
  43.2 0.4 convolution_convert_fusion
  43.7 0.3 fusion.39
  44.0 0.3 copy.35
  44.3 0.9 %copy.40 = bf16[12,192,4,32]{1,3,0,2:T(8,128)(2,1)} copy(bf16[12,192,4,32]{1,3,2,0:T(8,128)(2,1)S(1)} %bitcast.59) | data formatting | bytes 1179648 | tf_op jit(solution)/shard_map/while | solution.py:67
  45.2 1.2 %copy.37 = bf16[12,192,128]{1,2,0:T(8,128)(2,1)} copy(bf16[12,192,128]{2,1,0:T(8,128)(2,1)S(1)} %get-tuple-element.188) | data formatting | bytes 1179648 | tf_op jit(solution)/shard_map/slice | solution.py:43
  46.4 0.3 fusion.28
  46.7 1.2 %copy.34 = bf16[12,192,128]{1,2,0:T(8,128)(2,1)} copy(bf16[12,192,128]{2,1,0:T(8,128)(2,1)S(1)} %fusion.28) | data formatting | bytes 1179648 | tf_op jit(solution)/shard_map/convert_element_type | solution.py:39
  47.9 1.5 %fusion.27 = f32[12,192,128]{2,1,0:T(8,128)} fusion(bf16[12,192,128]{2,1,0:T(8,128)(2,1)S(1)} %bitcast.58, f32[128]{0:T(128)S(1)} %copy-done.13, bf16[128,128]{1,0:T(8,128)(2,1)S(1)} %copy-done.11), kind=kOutput, calls=%fused_computation.29 | convolution fusion | flops 76677120 | bytes 1802752 | tf_op jit(solution)/shard_map/dot_general | solution.py:44
  49.3 1.0 %broadcast_in_dim.45.clone = bf16[12,192,128]{2,0,1:T(8,128)(2,1)} broadcast(bf16[]{:T(256)} %constant.57.clone.1), dimensions={} | broadcast | bytes 589826 | tf_op jit(solution)/shard_map/broadcast_in_dim | solution.py:71
  50.3 18.9 %while.13 = (s32[]{:T(128)}, bf16[12,192,128]{2,0,1:T(8,128)(2,1)}, f32[12,192,128]{2,1,0:T(8,128)}, pred[192]{0:T(512)(128)(4,1)S(1)}, bf16[12,192,4,32]{1,3,2,...) while((s32[]{:T(128)}, bf16[12,192,128]{2,0,1:T(8,128)(2,1)}, ...), condition=%wide.region_5.6_spmd, body=%wide.region_2.5_spmd.sunk | while | flops 118112448 | bytes 19440052 | solution.py:67
  50.3 0.3 constant_dynamic-slice_fusion.13
  50.8 4.4 %fusion.59 = (f32[4,12,96]{2,1,0:T(8,128)S(1)}, bf16[4,12,96,192]{3,2,1,0:T(8,128)(2,1)}) fusion(f32[4,96,192]{2,1,0:T(8,128)S(1)} %copy.78, pred[192]{0:T(512)(128)(4,1)S(1)} %get-tuple-element.270, bf16[12,192,4,32]{1,3,0,2:T(8,128)(2,1)S(1)} %get-tuple-element.272, bf16[12,192,4,32]{1,3,2,0:T(8,128)(2,1)} %get-tuple-element.271, s32[]{:T(128)S(6)} %select_n.31), kind=kOutput, calls=%fused_computation.43.clone.1 | convolution fusion | flops 61046976 | bytes 3066052 | tf_op jit(solution)/shard_map/while/body/eval_jaxpr/sub | solution.py:59
  55.3 2.9 %fusion.60 = f32[12,96,4,32]{1,3,2,0:T(8,128)S(1)} fusion(bf16[12,192,4,32]{1,3,2,0:T(8,128)(2,1)} %get-tuple-element.274, bf16[4,12,96,192]{3,2,1,0:T(8,128)(2,1)} %get-tuple-element.241, f32[12,96,4]{1,2,0:T(4,128)S(1)} %copy.79), kind=kOutput, calls=%fused_computation.10.clone.1 | convolution fusion | flops 56770560 | bytes 2967552 | tf_op jit(solution)/shard_map/while/body/eval_jaxpr/hijk,ikhd->ijhd/dot_general | solution.py:62
  58.3 0.3 copy.77
  58.6 0.3 copy.80
  59.0 0.8 constant_dynamic-update-slice_fusion.2
  59.8 0.3 constant_dynamic-slice_fusion.13
  60.3 4.4 %fusion.59 = (f32[4,12,96]{2,1,0:T(8,128)S(1)}, bf16[4,12,96,192]{3,2,1,0:T(8,128)(2,1)}) fusion(f32[4,96,192]{2,1,0:T(8,128)S(1)} %copy.78, pred[192]{0:T(512)(128)(4,1)S(1)} %get-tuple-element.270, bf16[12,192,4,32]{1,3,0,2:T(8,128)(2,1)S(1)} %get-tuple-element.272, bf16[12,192,4,32]{1,3,2,0:T(8,128)(2,1)} %get-tuple-element.271, s32[]{:T(128)S(6)} %select_n.31), kind=kOutput, calls=%fused_computation.43.clone.1 | convolution fusion | flops 61046976 | bytes 3066052 | tf_op jit(solution)/shard_map/while/body/eval_jaxpr/sub | solution.py:59
  64.7 2.9 %fusion.60 = f32[12,96,4,32]{1,3,2,0:T(8,128)S(1)} fusion(bf16[12,192,4,32]{1,3,2,0:T(8,128)(2,1)} %get-tuple-element.274, bf16[4,12,96,192]{3,2,1,0:T(8,128)(2,1)} %get-tuple-element.241, f32[12,96,4]{1,2,0:T(4,128)S(1)} %copy.79), kind=kOutput, calls=%fused_computation.10.clone.1 | convolution fusion | flops 56770560 | bytes 2967552 | tf_op jit(solution)/shard_map/while/body/eval_jaxpr/hijk,ikhd->ijhd/dot_general | solution.py:62
  68.1 0.3 copy.80
  68.4 0.8 constant_dynamic-update-slice_fusion.2
  69.2 15.2 %all_to_all.36 = bf16[12,192,128]{2,0,1:T(8,128)(2,1)S(1)} all-to-all(bf16[12,192,128]{2,0,1:T(8,128)(2,1)} %get-tuple-element.281), channel_id=1, replica_groups=mesh['groups'=2,'rows'=4,'cols'=4] {'rows'}, dimensions={1} | all-to-all | bytes 1179648 | tf_op jit(solution)/shard_map/all_to_all | solution.py:73
  84.6 1.3 %convolution_add_fusion = f32[48,48,128]{2,1,0:T(8,128)} fusion(bf16[48,48,128]{2,1,0:T(8,128)(2,1)S(1)} %bitcast.62, f32[128]{0:T(128)S(1)} %copy-done.10, bf16[128,128]{1,0:T(8,128)(2,1)S(1)} %copy-done.5), kind=kOutput, calls=%fused_computation.23 | convolution fusion | flops 75792384 | bytes 1802752 | tf_op jit(solution)/shard_map/dot_general | solution.py:74
  (52 shorter events, 1.6 us)
Async XLA Ops:
  0.0 43.2 %copy-start = (bf16[128,256]{1,0:T(8,128)(2,1)S(1)}, bf16[128,256]{1,0:T(8,128)(2,1)}, u32[]{:S(2)}) copy-start(bf16[128,256]{1,0:T(8,128)(2,1)} %param.18) | copy-start | bytes 196612
  0.0 1.8 %copy-start.1 = (f32[48,48,128]{2,1,0:T(8,128)S(1)}, f32[48,48,128]{2,1,0:T(8,128)}, u32[]{:S(2)}) copy-start(f32[48,48,128]{2,1,0:T(8,128)} %param.13) | copy-start | bytes 3538948
  0.0 2.5 %copy-start.9 = (f32[128]{0:T(128)S(1)}, f32[128]{0:T(128)}, u32[]{:S(2)}) copy-start(f32[128]{0:T(128)} %param.15) | copy-start | bytes 1540
  0.0 2.5 %copy-start.8 = (f32[128]{0:T(128)S(1)}, f32[128]{0:T(128)}, u32[]{:S(2)}) copy-start(f32[128]{0:T(128)} %param.16) | copy-start | bytes 1540
  2.5 5.8 %copy-start.7 = (f32[128,4]{0,1:T(4,128)S(1)}, f32[128,4]{0,1:T(4,128)}, u32[]{:S(2)}) copy-start(f32[128,4]{0,1:T(4,128)} %param.21) | copy-start | bytes 6148
  4.0 39.1 %all-to-all-start = ((bf16[48,48,128]{2,1,0:T(8,128)(2,1)}), bf16[48,48,128]{2,1,0:T(8,128)(2,1)S(1)}, u32[]{:S(2)}, u32[]{:S(2)}) async-start(bf16[48,48,128]{2,1,0:T(8,128)(2,1)} %add_convert_fusion), calls=%async_computation | async-start | bytes 1179648 | tf_op jit(solution)/shard_map/all_to_all | solution.py:30
  8.3 18.9 %copy-start.14 = (u32[32]{0:T(128)S(1)}, u32[32]{0:T(128)}, u32[]{:S(2)}) copy-start(u32[32]{0:T(128)} %constant.66) | copy-start | bytes 388
  8.3 20.1 %copy-start.12 = (s32[48]{0:T(128)S(1)}, s32[48]{0:T(128)}, u32[]{:S(2)}) copy-start(s32[48]{0:T(128)} %param.14) | copy-start | bytes 580
  44.3 2.1 %copy-start.6 = (bf16[128,128]{1,0:T(8,128)(2,1)S(1)}, bf16[128,128]{1,0:T(8,128)(2,1)}, u32[]{:S(2)}) copy-start(bf16[128,128]{1,0:T(8,128)(2,1)} %param.17) | copy-start | bytes 98308
  46.4 1.5 %copy-start.11 = (bf16[128,128]{1,0:T(8,128)(2,1)S(1)}, bf16[128,128]{1,0:T(8,128)(2,1)}, u32[]{:S(2)}) copy-start(bf16[128,128]{1,0:T(8,128)(2,1)} %param.19) | copy-start | bytes 98308
  46.4 1.5 %copy-start.13 = (f32[128]{0:T(128)S(1)}, f32[128]{0:T(128)}, u32[]{:S(2)}) copy-start(f32[128]{0:T(128)} %param.20) | copy-start | bytes 1540
  47.9 2.5 %copy-start.3 = (bf16[12,192,4,32]{1,3,0,2:T(8,128)(2,1)S(1)}, bf16[12,192,4,32]{1,3,0,2:T(8,128)(2,1)}, u32[]{:S(2)}) copy-start(bf16[12,192,4,32]{1,3,0,2:T(8,128)(2,1)} %copy.40) | copy-start | bytes 1769476
  55.3 2.9 %copy-start.2 = (f32[12,192,128]{2,1,0:T(8,128)S(1)}, f32[12,192,128]{2,1,0:T(8,128)}, u32[]{:S(2)}) copy-start(f32[12,192,128]{2,1,0:T(8,128)} %get-tuple-element.269) | copy-start | bytes 3538948 | tf_op jit(solution)/shard_map/while
  58.6 1.2 %copy-start.4 = (bf16[12,192,4,32]{1,3,0,2:T(8,128)(2,1)S(1)}, bf16[12,192,4,32]{1,3,0,2:T(8,128)(2,1)}, u32[]{:S(2)}) copy-start(bf16[12,192,4,32]{1,3,0,2:T(8,128)(2,1)} %get-tuple-element.292) | copy-start | bytes 1769476 | tf_op jit(solution)/shard_map/while
  64.7 2.9 %copy-start.2 = (f32[12,192,128]{2,1,0:T(8,128)S(1)}, f32[12,192,128]{2,1,0:T(8,128)}, u32[]{:S(2)}) copy-start(f32[12,192,128]{2,1,0:T(8,128)} %get-tuple-element.269) | copy-start | bytes 3538948 | tf_op jit(solution)/shard_map/while
  68.1 1.1 %copy-start.4 = (bf16[12,192,4,32]{1,3,0,2:T(8,128)(2,1)S(1)}, bf16[12,192,4,32]{1,3,0,2:T(8,128)(2,1)}, u32[]{:S(2)}) copy-start(bf16[12,192,4,32]{1,3,0,2:T(8,128)(2,1)} %get-tuple-element.292) | copy-start | bytes 1769476 | tf_op jit(solution)/shard_map/while
  69.2 15.4 %copy-start.5 = (bf16[128,128]{1,0:T(8,128)(2,1)S(1)}, bf16[128,128]{1,0:T(8,128)(2,1)}, u32[]{:S(2)}) copy-start(bf16[128,128]{1,0:T(8,128)(2,1)} %param.22) | copy-start | bytes 98308
  69.2 15.4 %copy-start.10 = (f32[128]{0:T(128)S(1)}, f32[128]{0:T(128)}, u32[]{:S(2)}) copy-start(f32[128]{0:T(128)} %param.23) | copy-start | bytes 1540
where the time goes:
time: 86.4 us; the launch traced here: 85.9 us
  blocking collectives  45.7 us (53%)
  matrix products  21 us (24%)
  local copies, waits for them, and re-layouts  9.81 us (11%)
  other arithmetic  4.24 us (5%)
  starting transfers between devices  4.24 us (5%)
    all_gather x1, blocking collectives, whole_row_layer(): bias_part = lax.all_gather(local_bias, 'cols', axis=1, tiled=True)  15.8 us
    all_to_all x1, blocking collectives, whole_row_layer(): lax.all_to_all(gated_all, 'rows', split_axis=1, concat_axis=0, tiled=True)  15.2 us
    all_gather x1, blocking collectives, whole_row_layer(): lax.all_gather(bias_part, 'rows', axis=2, tiled=True)  9.04 us
    sub x2, matrix products, one_block(): expo = jnp.exp(scores - highest)  8.86 us
    dot_general x2, matrix products, one_block(): jnp.einsum('hijk,ikhd->ijhd', weights, values, preferred_element_type=jnp...  5.81 us
    unnamed x1, blocking collectives  5.63 us
    all_to_all x1, starting transfers between devices, whole_row_layer(): lax.all_to_all(normed, 'rows', split_axis=0, concat_axis=1, tiled=True)  4.24 us
    dot_general x1, matrix products, whole_row_layer(): jnp.dot(normed.astype(jnp.float32), w_bias, precision=lax.Precision.HIGHEST)  2.85 us
  transfers between devices with their start and end apart: 1, of which 0 were waited for; matrix products, arithmetic and copies ran while one was open for 4% of the time, Pallas kernels for 0%

commit v1 on v0

--- a/solution.py
+++ b/solution.py
@@ -5,6 +5,19 @@
 
 HEADS = 4
 HEAD_DIM = 32
+
+
+def register_the_tiles(arr):
+    which_axis = "cols"
+    k_all = lax.axis_size(which_axis)
+    formed = sorted(((q, (q + 1) % k_all) for q in range(k_all)))
+    z = arr
+    gallery = [z]
+    for hop_no in range(1, k_all):
+        z = lax.ppermute(z, axis_name=which_axis, perm=formed)
+        gallery.insert(0, z)
+    current_block = jnp.concatenate(gallery, axis=1)
+    return jnp.roll(current_block, shift=(lax.axis_index(which_axis) + 1) * arr.shape[1], axis=1)
 
 
 def layer_norm(values, norm_gain, norm_shift):
@@ -29,7 +42,7 @@
     ).transpose(2, 0, 1)
     wide = lax.all_to_all(normed, "rows", split_axis=0, concat_axis=1, tiled=True)
     few_rows, token_count, _ = wide.shape
-    bias_part = lax.all_gather(local_bias, "cols", axis=1, tiled=True)
+    bias_part = register_the_tiles(local_bias)
     full_bias, full_mask = (
         lax.all_gather(bias_part, "rows", axis=2, tiled=True),
         lax.all_gather(token_mask.astype(jnp.float32), "rows", axis=0, tiled=True),

time: 86.4 us -> 83.4 us (0.965)
  blocking collectives: 45.7 us -> 31.8 us
  starting transfers between devices: 4.24 us -> 9.76 us
  waiting for transfers between devices: 0.01 us -> 4.88 us
    all_gather x1 -> x0, blocking collectives: 15.8 us -> none  [whole_row_layer(): bias_part = lax.all_gather(local_bias, 'cols', axis=1, tiled=True)]
    ppermute x0 -> x3, starting transfers between devices: none -> 6.28 us  [register_the_tiles(): z = lax.ppermute(z, axis_name=which_axis, perm=formed)]
    ppermute x0 -> x3, waiting for transfers between devices: none -> 4.88 us  [register_the_tiles(): z = lax.ppermute(z, axis_name=which_axis, perm=formed)]
    unnamed x1, blocking collectives: 5.63 us -> 7.9 us
  transfers between devices with their start and end apart: 1 -> 4, of which waited for: 0 -> 1; matrix products, arithmetic and copies ran while one was open for 4% -> 1% of each run, Pallas kernels for 0% -> 0%
where the time goes in v1:
time: 83.4 us; the launch traced here: 82.9 us
  blocking collectives  31.8 us (38%)
  matrix products  21.1 us (25%)
  local copies, waits for them, and re-layouts  10.1 us (12%)
  starting transfers between devices  9.76 us (12%)
  waiting for transfers between devices  4.88 us (6%)
  other arithmetic  4.22 us (5%)
  between operations  0.95 us (1%)
    all_to_all x1, blocking collectives, whole_row_layer(): lax.all_to_all(gated_all, 'rows', split_axis=1, concat_axis=0, tiled=True)  15.2 us
    sub x2, matrix products, one_block(): expo = jnp.exp(scores - highest)  8.87 us
    all_gather x1, blocking collectives, whole_row_layer(): lax.all_gather(bias_part, 'rows', axis=2, tiled=True)  8.7 us
    unnamed x1, blocking collectives  7.9 us
    ppermute x3, starting transfers between devices, register_the_tiles(): z = lax.ppermute(z, axis_name=which_axis, perm=formed)  6.28 us
    dot_general x2, matrix products, one_block(): jnp.einsum('hijk,ikhd->ijhd', weights, values, preferred_element_type=jnp...  5.81 us
    ppermute x3, waiting for transfers between devices, register_the_tiles(): z = lax.ppermute(z, axis_name=which_axis, perm=formed)  4.88 us
    all_to_all x1, starting transfers between devices, whole_row_layer(): lax.all_to_all(normed, 'rows', split_axis=0, concat_axis=1, tiled=True)  3.48 us
  transfers between devices with their start and end apart: 4, of which 1 were waited for; matrix products, arithmetic and copies ran while one was open for 1% of the time, Pallas kernels for 0%

profile of v1, /device:TPU:0, one launch (start us, length us, event | category | flops | bytes accessed | tf_op | source)
XLA Modules:
  0.0 82.9 jit_solution(17491822389917839355)
XLA Ops:
  0.0 1.7 %reduce_sum.31 = f32[48,48]{1,0:T(8,128)S(1)} reduce(f32[48,48,128]{2,1,0:T(8,128)} %param.13, f32[]{:T(128)} %constant.79.clone.1), dimensions={2}, to_apply=%region_0.0 | reduce | flops 292608 | bytes 1188868 | tf_op jit(solution)/shard_map/reduce_sum | solution.py:24
  1.8 0.7 multiply_reduce_fusion
  2.5 1.5 %add_convert_fusion = bf16[48,48,128]{2,1,0:T(8,128)(2,1)} fusion(f32[48,48,128]{2,1,0:T(8,128)S(1)} %copy-done.1, f32[128]{0:T(128)S(1)} %copy-done.8, f32[128]{0:T(128)S(1)} %copy-done.9, f32[48,48]{1,0:T(8,128)S(1)} %add_rsqrt_fusion, f32[48,48]{1,0:T(8,128)S(1)} %broadcast_multiply_fusion), kind=kLoop, calls=%fused_computation.31 | loop fusion | flops 1474560 | bytes 1788928 | tf_op jit(solution)/shard_map/convert_element_type | solution.py:27
  4.0 2.9 %convolution_bitcast_fusion = f32[4,48,48]{2,0,1:T(4,128)S(1)} fusion(bf16[48,48,128]{2,1,0:T(8,128)(2,1)} %add_convert_fusion, f32[128,4]{0,1:T(4,128)S(1)} %copy-done.7), kind=kOutput, calls=%fused_computation.33 | convolution fusion | flops 14155776 | bytes 628736 | tf_op jit(solution)/shard_map/dot_general | solution.py:40
  6.9 3.1 %collective-permute-start = (f32[4,48,48]{2,0,1:T(4,128)S(1)}, f32[4,48,48]{2,0,1:T(4,128)S(1)}, u32[]{:S(2)}, u32[]{:S(2)}) collective-permute-start(f32[4,48,48]{2,0,1:T(4,128)S(1)} %convolution_bitcast_fusion), channel_id=1, source_target_pairs={{0,1},{1,2},{2,3},{3,0},{4,5},{5,6},{6,7},{7,4},{8,9},{9,10},{10,1... | collective-permute-start | bytes 110600 | tf_op jit(solution)/shard_map/ppermute | solution.py:17
  10.0 3.5 %all-to-all-start = ((bf16[48,48,128]{2,1,0:T(8,128)(2,1)}), bf16[48,48,128]{2,1,0:T(8,128)(2,1)S(1)}, u32[]{:S(2)}, u32[]{:S(2)}) async-start(bf16[48,48,128]{2,1,0:T(8,128)(2,1)} %add_convert_fusion), calls=%async_computation | async-start | bytes 1179648 | tf_op jit(solution)/shard_map/all_to_all | solution.py:43
  13.5 0.7 dynamic-slice
  14.8 1.6 %collective-permute-start.1 = (f32[4,48,48]{2,0,1:T(4,128)S(1)}, f32[4,48,48]{2,0,1:T(4,128)S(1)}, u32[]{:S(2)}, u32[]{:S(2)}) collective-permute-start(f32[4,48,48]{2,0,1:T(4,128)S(1)} %collective-permute-done), channel_id=1, source_target_pairs={{0,1},{1,2},{2,3},{3,0},{4,5},{5,6},{6,7},{7,4},{8,9},{9,10},{10,1... | collective-permute-start | bytes 110600 | tf_op jit(solution)/shard_map/ppermute | solution.py:17
  16.6 7.9 %all-reduce = f32[192]{0:T(256)S(1)} all-reduce(f32[192]{0:T(256)S(1)} %convert_dynamic-update-slice_fusion), channel_id=1, replica_groups=mesh['groups'=2,'rows'=4,'cols'=4] {'rows'}, use_global_device_ids=true, to_apply=%add | all-reduce | flops 192 | bytes 1536
  24.5 1.6 %collective-permute-start.2 = (f32[4,48,48]{2,0,1:T(4,128)S(1)}, f32[4,48,48]{2,0,1:T(4,128)S(1)}, u32[]{:S(2)}, u32[]{:S(2)}) collective-permute-start(f32[4,48,48]{2,0,1:T(4,128)S(1)} %collective-permute-done.1), channel_id=1, source_target_pairs={{0,1},{1,2},{2,3},{3,0},{4,5},{5,6},{6,7},{7,4},{8,9},{9,10},{10,1... | collective-permute-start | bytes 110600 | tf_op jit(solution)/shard_map/ppermute | solution.py:17
  26.0 4.9 %collective-permute-done.2 = f32[4,48,48]{2,0,1:T(4,128)S(1)} collective-permute-done((f32[4,48,48]{2,0,1:T(4,128)S(1)}, f32[4,48,48]{2,0,1:T(4,128)S(1)}, u32[]{:S(2)}, u32[]{:S(2)}) %collective-permute-start.2) | collective-permute-done | bytes 36896 | tf_op jit(solution)/shard_map/ppermute | solution.py:17
  31.3 8.7 %all_gather.7 = f32[4,192,192]{1,0,2:T(4,128)S(1)} all-gather(f32[4,192,48]{1,0,2:T(4,128)S(1)} %copy.58), channel_id=1, replica_groups=mesh['groups'=2,'rows'=4,'cols'=4] {'rows'}, dimensions={2}, use_global_device_ids=true | all-gather | bytes 737280 | tf_op jit(solution)/shard_map/all_gather | solution.py:47
  40.1 0.4 convolution_convert_fusion
  40.6 0.3 fusion.39
  40.9 0.3 copy.57
  41.2 1.0 %copy.62 = bf16[12,192,4,32]{1,3,0,2:T(8,128)(2,1)} copy(bf16[12,192,4,32]{1,3,2,0:T(8,128)(2,1)S(1)} %bitcast.59) | data formatting | bytes 1179648 | tf_op jit(solution)/shard_map/while | solution.py:80
  42.1 1.2 %copy.59 = bf16[12,192,128]{1,2,0:T(8,128)(2,1)} copy(bf16[12,192,128]{2,1,0:T(8,128)(2,1)S(1)} %get-tuple-element.196) | data formatting | bytes 1179648 | tf_op jit(solution)/shard_map/slice | solution.py:56
  43.3 0.3 fusion.28
  43.6 1.2 %copy.56 = bf16[12,192,128]{1,2,0:T(8,128)(2,1)} copy(bf16[12,192,128]{2,1,0:T(8,128)(2,1)S(1)} %fusion.28) | data formatting | bytes 1179648 | tf_op jit(solution)/shard_map/convert_element_type | solution.py:52
  44.8 1.5 %fusion.27 = f32[12,192,128]{2,1,0:T(8,128)} fusion(bf16[12,192,128]{2,1,0:T(8,128)(2,1)S(1)} %bitcast.58, f32[128]{0:T(128)S(1)} %copy-done.13, bf16[128,128]{1,0:T(8,128)(2,1)S(1)} %copy-done.11), kind=kOutput, calls=%fused_computation.29 | convolution fusion | flops 76677120 | bytes 1802752 | tf_op jit(solution)/shard_map/dot_general | solution.py:57
  46.3 1.0 %broadcast_in_dim.45.clone = bf16[12,192,128]{2,0,1:T(8,128)(2,1)} broadcast(bf16[]{:T(256)} %constant.78.clone.1), dimensions={} | broadcast | bytes 589826 | tf_op jit(solution)/shard_map/broadcast_in_dim | solution.py:84
  47.3 18.9 %while.13 = (s32[]{:T(128)}, bf16[12,192,128]{2,0,1:T(8,128)(2,1)}, f32[12,192,128]{2,1,0:T(8,128)}, pred[192]{0:T(512)(128)(4,1)S(1)}, bf16[12,192,4,32]{1,3,2,...) while((s32[]{:T(128)}, bf16[12,192,128]{2,0,1:T(8,128)(2,1)}, ...), condition=%wide.region_5.6_spmd, body=%wide.region_2.5_spmd.sunk | while | flops 118112448 | bytes 19440052 | solution.py:80
  47.8 4.4 %fusion.59 = (f32[4,12,96]{2,1,0:T(8,128)S(1)}, bf16[4,12,96,192]{3,2,1,0:T(8,128)(2,1)}) fusion(f32[4,96,192]{2,1,0:T(8,128)S(1)} %copy.100, pred[192]{0:T(512)(128)(4,1)S(1)} %get-tuple-element.278, bf16[12,192,4,32]{1,3,0,2:T(8,128)(2,1)S(1)} %get-tuple-element.280, bf16[12,192,4,32]{1,3,2,0:T(8,128)(2,1)} %get-tuple-element.279, s32[]{:T(128)S(6)} %select_n.46), kind=kOutput, calls=%fused_computation.52.clone.1 | convolution fusion | flops 61046976 | bytes 3066052 | tf_op jit(solution)/shard_map/while/body/eval_jaxpr/sub | solution.py:72
  52.3 2.9 %fusion.60 = f32[12,96,4,32]{1,3,2,0:T(8,128)S(1)} fusion(bf16[12,192,4,32]{1,3,2,0:T(8,128)(2,1)} %get-tuple-element.282, bf16[4,12,96,192]{3,2,1,0:T(8,128)(2,1)} %get-tuple-element.249, f32[12,96,4]{1,2,0:T(4,128)S(1)} %copy.101), kind=kOutput, calls=%fused_computation.10.clone.1 | convolution fusion | flops 56770560 | bytes 2967552 | tf_op jit(solution)/shard_map/while/body/eval_jaxpr/hijk,ikhd->ijhd/dot_general | solution.py:75
  55.6 0.3 copy.102
  56.0 0.8 constant_dynamic-update-slice_fusion.10
  57.3 4.4 %fusion.59 = (f32[4,12,96]{2,1,0:T(8,128)S(1)}, bf16[4,12,96,192]{3,2,1,0:T(8,128)(2,1)}) fusion(f32[4,96,192]{2,1,0:T(8,128)S(1)} %copy.100, pred[192]{0:T(512)(128)(4,1)S(1)} %get-tuple-element.278, bf16[12,192,4,32]{1,3,0,2:T(8,128)(2,1)S(1)} %get-tuple-element.280, bf16[12,192,4,32]{1,3,2,0:T(8,128)(2,1)} %get-tuple-element.279, s32[]{:T(128)S(6)} %select_n.46), kind=kOutput, calls=%fused_computation.52.clone.1 | convolution fusion | flops 61046976 | bytes 3066052 | tf_op jit(solution)/shard_map/while/body/eval_jaxpr/sub | solution.py:72
  61.7 2.9 %fusion.60 = f32[12,96,4,32]{1,3,2,0:T(8,128)S(1)} fusion(bf16[12,192,4,32]{1,3,2,0:T(8,128)(2,1)} %get-tuple-element.282, bf16[4,12,96,192]{3,2,1,0:T(8,128)(2,1)} %get-tuple-element.249, f32[12,96,4]{1,2,0:T(4,128)S(1)} %copy.101), kind=kOutput, calls=%fused_computation.10.clone.1 | convolution fusion | flops 56770560 | bytes 2967552 | tf_op jit(solution)/shard_map/while/body/eval_jaxpr/hijk,ikhd->ijhd/dot_general | solution.py:75
  65.1 0.3 copy.102
  65.4 0.8 constant_dynamic-update-slice_fusion.10
  66.2 15.2 %all_to_all.36 = bf16[12,192,128]{2,0,1:T(8,128)(2,1)S(1)} all-to-all(bf16[12,192,128]{2,0,1:T(8,128)(2,1)} %get-tuple-element.290), channel_id=1, replica_groups=mesh['groups'=2,'rows'=4,'cols'=4] {'rows'}, dimensions={1} | all-to-all | bytes 1179648 | tf_op jit(solution)/shard_map/all_to_all | solution.py:86
  81.6 1.3 %convolution_add_fusion = f32[48,48,128]{2,1,0:T(8,128)} fusion(bf16[48,48,128]{2,1,0:T(8,128)(2,1)S(1)} %bitcast.62, f32[128]{0:T(128)S(1)} %copy-done.10, bf16[128,128]{1,0:T(8,128)(2,1)S(1)} %copy-done.5), kind=kOutput, calls=%fused_computation.23 | convolution fusion | flops 75792384 | bytes 1802752 | tf_op jit(solution)/shard_map/dot_general | solution.py:87
  (66 shorter events, 2.5 us)
Async XLA Ops:
  0.0 40.1 %copy-start = (bf16[128,256]{1,0:T(8,128)(2,1)S(1)}, bf16[128,256]{1,0:T(8,128)(2,1)}, u32[]{:S(2)}) copy-start(bf16[128,256]{1,0:T(8,128)(2,1)} %param.18) | copy-start | bytes 196612
  0.0 1.8 %copy-start.1 = (f32[48,48,128]{2,1,0:T(8,128)S(1)}, f32[48,48,128]{2,1,0:T(8,128)}, u32[]{:S(2)}) copy-start(f32[48,48,128]{2,1,0:T(8,128)} %param.13) | copy-start | bytes 3538948
  0.0 2.5 %copy-start.9 = (f32[128]{0:T(128)S(1)}, f32[128]{0:T(128)}, u32[]{:S(2)}) copy-start(f32[128]{0:T(128)} %param.15) | copy-start | bytes 1540
  0.0 2.5 %copy-start.8 = (f32[128]{0:T(128)S(1)}, f32[128]{0:T(128)}, u32[]{:S(2)}) copy-start(f32[128]{0:T(128)} %param.16) | copy-start | bytes 1540
  2.5 1.6 %copy-start.7 = (f32[128,4]{0,1:T(4,128)S(1)}, f32[128,4]{0,1:T(4,128)}, u32[]{:S(2)}) copy-start(f32[128,4]{0,1:T(4,128)} %param.21) | copy-start | bytes 6148
  4.0 9.4 %copy-start.14 = (u32[32]{0:T(128)S(1)}, u32[32]{0:T(128)}, u32[]{:S(2)}) copy-start(u32[32]{0:T(128)} %constant.92) | copy-start | bytes 388
  4.0 12.4 %copy-start.12 = (s32[48]{0:T(128)S(1)}, s32[48]{0:T(128)}, u32[]{:S(2)}) copy-start(s32[48]{0:T(128)} %param.14) | copy-start | bytes 580
  6.9 7.9 %collective-permute-start = (f32[4,48,48]{2,0,1:T(4,128)S(1)}, f32[4,48,48]{2,0,1:T(4,128)S(1)}, u32[]{:S(2)}, u32[]{:S(2)}) collective-permute-start(f32[4,48,48]{2,0,1:T(4,128)S(1)} %convolution_bitcast_fusion), channel_id=1, source_target_pairs={{0,1},{1,2},{2,3},{3,0},{4,5},{5,6},{6,7},{7,4},{8,9},{9,10},{10,1... | collective-permute-start | bytes 110600 | tf_op jit(solution)/shard_map/ppermute | solution.py:17
  10.0 30.1 %all-to-all-start = ((bf16[48,48,128]{2,1,0:T(8,128)(2,1)}), bf16[48,48,128]{2,1,0:T(8,128)(2,1)S(1)}, u32[]{:S(2)}, u32[]{:S(2)}) async-start(bf16[48,48,128]{2,1,0:T(8,128)(2,1)} %add_convert_fusion), calls=%async_computation | async-start | bytes 1179648 | tf_op jit(solution)/shard_map/all_to_all | solution.py:43
  14.8 9.6 %collective-permute-start.1 = (f32[4,48,48]{2,0,1:T(4,128)S(1)}, f32[4,48,48]{2,0,1:T(4,128)S(1)}, u32[]{:S(2)}, u32[]{:S(2)}) collective-permute-start(f32[4,48,48]{2,0,1:T(4,128)S(1)} %collective-permute-done), channel_id=1, source_target_pairs={{0,1},{1,2},{2,3},{3,0},{4,5},{5,6},{6,7},{7,4},{8,9},{9,10},{10,1... | collective-permute-start | bytes 110600 | tf_op jit(solution)/shard_map/ppermute | solution.py:17
  24.5 6.5 %collective-permute-start.2 = (f32[4,48,48]{2,0,1:T(4,128)S(1)}, f32[4,48,48]{2,0,1:T(4,128)S(1)}, u32[]{:S(2)}, u32[]{:S(2)}) collective-permute-start(f32[4,48,48]{2,0,1:T(4,128)S(1)} %collective-permute-done.1), channel_id=1, source_target_pairs={{0,1},{1,2},{2,3},{3,0},{4,5},{5,6},{6,7},{7,4},{8,9},{9,10},{10,1... | collective-permute-start | bytes 110600 | tf_op jit(solution)/shard_map/ppermute | solution.py:17
  41.2 2.2 %copy-start.6 = (bf16[128,128]{1,0:T(8,128)(2,1)S(1)}, bf16[128,128]{1,0:T(8,128)(2,1)}, u32[]{:S(2)}) copy-start(bf16[128,128]{1,0:T(8,128)(2,1)} %param.17) | copy-start | bytes 98308
  43.3 1.5 %copy-start.11 = (bf16[128,128]{1,0:T(8,128)(2,1)S(1)}, bf16[128,128]{1,0:T(8,128)(2,1)}, u32[]{:S(2)}) copy-start(bf16[128,128]{1,0:T(8,128)(2,1)} %param.19) | copy-start | bytes 98308
  43.3 1.5 %copy-start.13 = (f32[128]{0:T(128)S(1)}, f32[128]{0:T(128)}, u32[]{:S(2)}) copy-start(f32[128]{0:T(128)} %param.20) | copy-start | bytes 1540
  44.8 2.5 %copy-start.3 = (bf16[12,192,4,32]{1,3,0,2:T(8,128)(2,1)S(1)}, bf16[12,192,4,32]{1,3,0,2:T(8,128)(2,1)}, u32[]{:S(2)}) copy-start(bf16[12,192,4,32]{1,3,0,2:T(8,128)(2,1)} %copy.62) | copy-start | bytes 1769476
  52.3 2.9 %copy-start.2 = (f32[12,192,128]{2,1,0:T(8,128)S(1)}, f32[12,192,128]{2,1,0:T(8,128)}, u32[]{:S(2)}) copy-start(f32[12,192,128]{2,1,0:T(8,128)} %get-tuple-element.277) | copy-start | bytes 3538948 | tf_op jit(solution)/shard_map/while
  55.6 1.2 %copy-start.4 = (bf16[12,192,4,32]{1,3,0,2:T(8,128)(2,1)S(1)}, bf16[12,192,4,32]{1,3,0,2:T(8,128)(2,1)}, u32[]{:S(2)}) copy-start(bf16[12,192,4,32]{1,3,0,2:T(8,128)(2,1)} %get-tuple-element.301) | copy-start | bytes 1769476 | tf_op jit(solution)/shard_map/while
  61.7 2.9 %copy-start.2 = (f32[12,192,128]{2,1,0:T(8,128)S(1)}, f32[12,192,128]{2,1,0:T(8,128)}, u32[]{:S(2)}) copy-start(f32[12,192,128]{2,1,0:T(8,128)} %get-tuple-element.277) | copy-start | bytes 3538948 | tf_op jit(solution)/shard_map/while
  65.1 1.2 %copy-start.4 = (bf16[12,192,4,32]{1,3,0,2:T(8,128)(2,1)S(1)}, bf16[12,192,4,32]{1,3,0,2:T(8,128)(2,1)}, u32[]{:S(2)}) copy-start(bf16[12,192,4,32]{1,3,0,2:T(8,128)(2,1)} %get-tuple-element.301) | copy-start | bytes 1769476 | tf_op jit(solution)/shard_map/while
  66.2 15.4 %copy-start.5 = (bf16[128,128]{1,0:T(8,128)(2,1)S(1)}, bf16[128,128]{1,0:T(8,128)(2,1)}, u32[]{:S(2)}) copy-start(bf16[128,128]{1,0:T(8,128)(2,1)} %param.22) | copy-start | bytes 98308
  66.2 15.4 %copy-start.10 = (f32[128]{0:T(128)S(1)}, f32[128]{0:T(128)}, u32[]{:S(2)}) copy-start(f32[128]{0:T(128)} %param.23) | copy-start | bytes 1540
